TPU v7x, 32 devices: a whole 2x2x4 slice. The times are simulated.
32 devices in a mesh: groups: 2 (over x), tile: 16 (over z, y, core).
Axes of the slice: x: 2, y: 2, z: 4, core: 2. Of those that a mesh axis runs over, the one named last changes fastest.
Arguments:
- grid_tokens: bfloat16 [16384, 512], P(('groups', 'tile')), parts along dimension 0, may hold values from -220 to 220
- obs_features: bfloat16 [65536, 128], P(('groups', 'tile')), parts along dimension 0, may hold values from -45 to 45
- w_obs: bfloat16 [128, 512], replicated, may hold values from -0.5 to 0.5
- b_obs: float32 [512], replicated, may hold values from -4 to 4
- w_query: bfloat16 [512, 512], replicated, may hold values from -0.25 to 0.25
- w_key: bfloat16 [512, 512], replicated, may hold values from -0.25 to 0.25
- w_value: bfloat16 [512, 512], replicated, may hold values from -0.25 to 0.25
- w_out: bfloat16 [512, 512], replicated, may hold values from -0.25 to 0.25
- block_lists: int32 [128, 32], P('groups'), parts along dimension 0, may hold values from 0 to 511, as said below
- block_counts: int32 [128], P('groups'), parts along dimension 0, may hold values from 24 to 32, as said below
- block_position: int32 [1024], P('groups'), parts along dimension 0, may hold values from 0 to 511, as said below
- proc_order: int32 [128], P('groups'), parts along dimension 0, may hold values from 0 to 63, each once
Outputs:
- arranged: bfloat16 [16384, 512], P(('groups', 'tile')), parts along dimension 0
There are 2 independent parts, one for each index of `groups`. A program takes and returns all parts, laid end to end along the dimension named above; an argument that names none is the same for every part. Nothing has to cross between parts.
Inputs may be any that keep to these rules, and one draw needn't show every extreme that they name: `block_lists`: over the entries below block_counts of the 4 tiles t of one device (t // 4 equal), at most 16 name blocks whose storage position // 32 is any one device; in every draw some device has exactly 16 from some device. `block_counts`: some tile uses all 32 entries. `block_position`: A permutation of the storage positions.
All inputs are finite; a program needn't handle non-finite values.
Results may differ from a plain program's by a relative error of at most 0.012.
The roundings to bfloat16 on the way count: a program that leaves them out, or rounds other values in their place, can miss the bound.
Values may be sent and summed in bfloat16 or wider, within the bound.
A program may use at most 128 MiB of HBM per device.

v0:
```python
import jax
import jax.numpy as jnp
from jax import lax
from jax.sharding import PartitionSpec as P

HEADS = 8
BLOCK = 64
NSEL = 32
TILE_ROWS = 128


def embed_rows(feats, feat_mean, feat_rstd, w_obs, b_obs):
    normed = ((feats.astype(jnp.float32) - feat_mean) * feat_rstd).astype(jnp.bfloat16)
    hidden = jnp.dot(normed, w_obs, preferred_element_type=jnp.float32) + b_obs
    return jax.nn.gelu(hidden, approximate=True).astype(jnp.bfloat16)


def local(
    grid_tokens,
    obs_features,
    w_obs,
    b_obs,
    w_query,
    w_key,
    w_value,
    w_out,
    block_lists,
    block_counts,
    block_position,
    proc_order,
):
    tile_count = lax.axis_size("tile")
    own_index = lax.axis_index("tile")
    obs_blocks = obs_features.shape[0] // BLOCK
    tile_local = grid_tokens.shape[0] // TILE_ROWS
    entry_count = tile_local * NSEL
    capacity = max(2, 2 * entry_count // tile_count)
    width = grid_tokens.shape[1]
    obs_wide = obs_features.astype(jnp.float32)
    first_sum, second_sum = lax.psum(
        (jnp.sum(obs_wide, axis=0), jnp.sum(obs_wide * obs_wide, axis=0)), "tile"
    )
    obs_total = obs_features.shape[0] * tile_count
    feat_mean = first_sum / obs_total
    feat_rstd = lax.rsqrt(second_sum / obs_total - feat_mean * feat_mean + 1e-05)
    spots = jnp.take(block_position, block_lists, axis=0)
    is_valid = jnp.arange(NSEL, dtype=jnp.int32)[None, :] < block_counts[:, None]
    owner_dev = (spots // obs_blocks).reshape(tile_count, entry_count)
    local_blk = (spots % obs_blocks).reshape(tile_count, entry_count)
    valid_rows = is_valid.reshape(tile_count, entry_count)
    entry_order = jnp.arange(entry_count, dtype=jnp.int32)
    earlier = (
        (owner_dev[:, :, None] == owner_dev[:, None, :])
        & valid_rows[:, None, :]
        & (entry_order[None, :] < entry_order[:, None])[None, :, :]
    )
    slot_rank = jnp.sum(earlier.astype(jnp.int32), axis=2)
    mine = valid_rows & (owner_dev == own_index)
    slot_ids = jnp.arange(capacity, dtype=jnp.int32)
    hits = mine[:, None, :] & (slot_rank[:, None, :] == slot_ids[None, :, None])
    present = jnp.any(hits, axis=2)
    slot_block = jnp.sum(jnp.where(hits, local_blk[:, None, :], 0), axis=2)
    my_owner = lax.dynamic_index_in_dim(owner_dev, own_index, 0, keepdims=False)
    my_rank = lax.dynamic_index_in_dim(slot_rank, own_index, 0, keepdims=False)
    my_valid = lax.dynamic_index_in_dim(valid_rows, own_index, 0, keepdims=False)
    pick_slot = jnp.where(my_valid, my_owner * capacity + my_rank, 0)
    raw_blocks = obs_features.reshape(obs_blocks, BLOCK, obs_features.shape[1])
    chosen = jnp.take(raw_blocks, slot_block, axis=0)
    incoming = lax.all_to_all(
        jnp.where(present[:, :, None, None], chosen, jnp.zeros((), raw_blocks.dtype)),
        "tile",
        split_axis=0,
        concat_axis=0,
        tiled=True,
    )
    flat_blocks = incoming.reshape(tile_count * capacity, BLOCK, incoming.shape[3])
    chosen_rows = embed_rows(
        jnp.take(flat_blocks, pick_slot, axis=0).reshape(entry_count * BLOCK, incoming.shape[3]),
        feat_mean,
        feat_rstd,
        w_obs,
        b_obs,
    )
    key_rows = jnp.dot(chosen_rows, w_key, preferred_element_type=jnp.float32).astype(jnp.bfloat16)
    value_rows = jnp.dot(chosen_rows, w_value, preferred_element_type=jnp.float32).astype(
        jnp.bfloat16
    )
    query_rows = jnp.dot(grid_tokens, w_query, preferred_element_type=jnp.float32).astype(
        jnp.bfloat16
    )
    my_counts = lax.dynamic_slice_in_dim(block_counts, own_index * tile_local, tile_local)
    head_dim = width // HEADS
    scale = 1.0 / head_dim**0.5
    key_span = NSEL * BLOCK
    results = []
    for tile_pos in range(tile_local):
        query_tile = query_rows[tile_pos * TILE_ROWS : (tile_pos + 1) * TILE_ROWS]
        key_tile = key_rows[tile_pos * key_span : (tile_pos + 1) * key_span]
        value_tile = value_rows[tile_pos * key_span : (tile_pos + 1) * key_span]
        keymask = jnp.repeat(jnp.arange(NSEL, dtype=jnp.int32) < my_counts[tile_pos], BLOCK)

        def one_head(
            head, query_tile=query_tile, key_tile=key_tile, value_tile=value_tile, keymask=keymask
        ):
            query_head = lax.dynamic_slice_in_dim(query_tile, head * head_dim, head_dim, 1)
            key_head = lax.dynamic_slice_in_dim(key_tile, head * head_dim, head_dim, 1)
            value_head = lax.dynamic_slice_in_dim(value_tile, head * head_dim, head_dim, 1)
            scores = (
                lax.dot_general(
                    query_head,
                    key_head,
                    (((1,), (1,)), ((), ())),
                    preferred_element_type=jnp.float32,
                )
                * scale
            )
            scores = jnp.where(keymask[None, :], scores, jnp.float32(-1e30))
            peak = jnp.max(scores, axis=-1, keepdims=True)
            expo = jnp.exp(scores - peak)
            totals = jnp.sum(expo, axis=-1, keepdims=True)
            weights_bf = expo.astype(jnp.bfloat16)
            return jnp.dot(weights_bf, value_head, preferred_element_type=jnp.float32) / totals

        per_head = lax.map(one_head, jnp.arange(HEADS, dtype=jnp.int32))
        results.append(
            jnp.transpose(per_head, (1, 0, 2)).reshape(TILE_ROWS, width).astype(jnp.bfloat16)
        )
    attended = jnp.concatenate(results, axis=0)
    encoded = jnp.dot(attended, w_out, preferred_element_type=jnp.float32).astype(jnp.bfloat16)
    outgoing = encoded.reshape(tile_local, tile_count, TILE_ROWS // tile_count, width)
    arrived = lax.all_to_all(outgoing, "tile", split_axis=1, concat_axis=0, tiled=True)
    arrived = arrived.reshape(tile_count * tile_local, TILE_ROWS // tile_count, width)
    return jnp.take(arrived, proc_order, axis=0).reshape(
        tile_count * tile_local * (TILE_ROWS // tile_count), width
    )


def solution(mesh):
    in_specs = (
        P(("groups", "tile"), None),
        P(("groups", "tile"), None),
        P(),
        P(),
        P(),
        P(),
        P(),
        P(),
        P("groups", None),
        P("groups"),
        P("groups"),
        P("groups"),
    )
    out_specs = P(("groups", "tile"), None)
    return jax.shard_map(local, mesh=mesh, in_specs=in_specs, out_specs=out_specs, check_vma=False)
```

profile of v0, /device:TPU:13, one launch (start us, length us, event | category | flops | bytes accessed | tf_op | source)
XLA Modules:
  0.0 352.6 jit_solution(3823423452104202265)
XLA Ops:
  1.0 13.2 %gather_fusion = s32[2048]{0:T(1024)S(1)} fusion(s32[512]{0:T(512)S(1)} %copy-done.2, s32[2048]{0:T(1024)S(1)} %broadcast_clamp_fusion), kind=kCustom, calls=%fused_computation | custom fusion | bytes 24576 | tf_op jit(solution)/shard_map/jit(_take)/gather | solution.py:46
  16.2 3.1 gather_fusion.1
  19.3 3.9 %select_select_fusion = bf16[16,16,64,128]{3,2,1,0:T(8,128)(2,1)} fusion(bf16[16,16,64,128]{3,2,1,0:T(8,128)(2,1)} %bitcast.84, pred[16,16]{1,0:T(8,128)(4,1)S(1)} %compare_and_fusion, pred[16,16]{1,0:T(8,128)(4,1)S(1)} %fusion.75), kind=kLoop, calls=%fused_computation.76 | loop fusion | flops 4194304 | bytes 8389120 | tf_op jit(solution)/shard_map/jit(_where)/select_n | solution.py:70
  23.2 6.7 %all-to-all-start = ((bf16[16,16,64,128]{3,2,1,0:T(8,128)(2,1)}), bf16[16,16,64,128]{3,2,1,0:T(8,128)(2,1)}, u32[]{:S(2)}, u32[]{:S(2)}) async-start(bf16[16,16,64,128]{3,2,1,0:T(8,128)(2,1)} %select_select_fusion), calls=%async_computation | async-start | bytes 8388608 | tf_op jit(solution)/shard_map/all_to_all | solution.py:69
  30.4 108.5 %all-reduce = (f32[128]{0:T(128)S(1)}, f32[128]{0:T(128)S(1)}) all-reduce(f32[128]{0:T(128)S(1)} %get-tuple-element.226, f32[128]{0:T(128)S(1)} %get-tuple-element.225), channel_id=1, replica_groups=mesh['groups'=2,'tile'=16] {'tile'}, use_global_device_ids=true, to_apply=%region_6.7 | all-reduce | flops 256 | bytes 2048 | tf_op jit(solution)/shard_map/psum | solution.py:40
  142.5 3.2 gather_fusion.2
  145.7 4.3 %bitcast_select_fusion = bf16[8192,128]{1,0:T(8,128)(2,1)S(1)} fusion(bf16[128,64,128]{2,1,0:T(8,128)(2,1)S(1)} %gather_fusion.2, pred[8192]{0:T(1024)(128)(4,1)S(1)} %broadcast_in_dim.178), kind=kLoop, calls=%fused_computation.77 | loop fusion | flops 1048576 | bytes 4202496 | tf_op jit(solution)/shard_map/jit(_take)/select_n | solution.py:78
  150.0 6.6 %fusion.63 = bf16[8192,512]{1,0:T(8,128)(2,1)S(1)} fusion(bf16[128,512]{1,0:T(8,128)(2,1)S(1)} %copy-done.8, f32[512]{0:T(512)S(1)} %copy-done.9, bf16[8192,128]{1,0:T(8,128)(2,1)S(1)} %bitcast_select_fusion, f32[128]{0:T(128)S(1)} %get-tuple-element.315, f32[128]{0:T(128)S(1)} %get-tuple-element.314), kind=kOutput, calls=%fused_computation.72 | convolution fusion | flops 1119879168 | bytes 10619904 | tf_op jit(solution)/shard_map/dot_general | solution.py:14
  156.6 3.2 copy-done.11
  159.8 4.7 %convolution_convert_fusion = bf16[8192,512]{1,0:T(8,128)(2,1)S(1)} fusion(bf16[8192,512]{1,0:T(8,128)(2,1)S(1)} %fusion.63, bf16[512,512]{1,0:T(8,128)(2,1)S(1)} %copy-done), kind=kOutput, calls=%fused_computation.73 | convolution fusion | flops 4299161600 | bytes 17301504 | tf_op jit(solution)/shard_map/dot_general | solution.py:85
  164.6 8.1 %convolution_convert_fusion.1 = bf16[8192,512]{1,0:T(8,128)(2,1)S(1)} fusion(bf16[8192,512]{1,0:T(8,128)(2,1)} %copy-done.11, bf16[512,512]{1,0:T(8,128)(2,1)S(1)} %copy-done.7), kind=kOutput, calls=%fused_computation.74 | convolution fusion | flops 4299161600 | bytes 17301504 | tf_op jit(solution)/shard_map/dot_general | solution.py:84
  172.7 5.2 %fusion.86 = (bf16[2048,512]{1,0:T(8,128)(2,1)}, bf16[2048,512]{1,0:T(8,128)(2,1)S(1)}, bf16[2048,512]{1,0:T(8,128)(2,1)}, bf16[2048,512]{1,0:T(8,128)(2,1)}, bf...) fusion(bf16[8192,512]{1,0:T(8,128)(2,1)S(1)} %convolution_conver, ...), kind=kLoop, calls=%fused_computation.140 | loop fusion | bytes 33554432 | tf_op jit(solution)/shard_map/slice | solution.py:99
  177.9 40.6 %while.44 = (s32[]{:T(128)}, bf16[8,128,64]{1,2,0:T(8,128)(2,1)S(1)}, s32[8]{0:T(128)S(1)}, bf16[128,512]{1,0:T(8,128)(2,1)S(1)}, bf16[2048,512]{1,0:T(8,128)(2,...) while((s32[]{:T(128)}, ...), condition=%wide.region_10.11_spmd.clone, body=%wide.region_7.10_spmd.clone.sunk | while | flops 68951808 | bytes 4272331 | solution.py:124
  181.3 1.7 fusion.122
  218.5 40.2 %while.45 = (s32[]{:T(128)}, bf16[8,128,64]{1,2,0:T(8,128)(2,1)S(1)}, s32[8]{0:T(128)S(1)}, bf16[128,512]{1,0:T(8,128)(2,1)S(1)}, bf16[2048,512]{1,0:T(8,128)(2,...) while((s32[]{:T(128)}, ...), condition=%wide.region_14.15_spmd.clone, body=%wide.region_11.14_spmd.clone.sunk | while | flops 68951808 | bytes 4272331 | solution.py:124
  221.8 1.7 fusion.127
  258.8 39.2 %while.46 = (s32[]{:T(128)}, bf16[8,128,64]{1,2,0:T(8,128)(2,1)S(1)}, s32[8]{0:T(128)S(1)}, bf16[128,512]{1,0:T(8,128)(2,1)S(1)}, bf16[2048,512]{1,0:T(8,128)(2,...) while((s32[]{:T(128)}, ...), condition=%wide.region_18.19_spmd.clone, body=%wide.region_15.18_spmd.clone.sunk | while | flops 68951808 | bytes 4272331 | solution.py:124
  262.2 1.7 fusion.132
  267.1 1.7 fusion.132
  271.9 1.7 fusion.132
  276.8 1.7 fusion.132
  298.1 31.1 %while.47 = (s32[]{:T(128)}, bf16[8,128,64]{1,2,0:T(8,128)(2,1)S(1)}, s32[8]{0:T(128)S(1)}, bf16[128,512]{1,0:T(8,128)(2,1)S(1)}, bf16[2048,512]{1,0:T(8,128)(2,...) while((s32[]{:T(128)}, ...), condition=%wide.region_22.23_spmd.clone, body=%wide.region_19.22_spmd.clone.sunk | while | flops 68951808 | bytes 4271823 | solution.py:124
  331.6 5.9 %all-to-all-start.1 = ((bf16[4,16,8,512]{3,2,0,1:T(8,128)(2,1)}), bf16[4,16,8,512]{3,2,0,1:T(8,128)(2,1)S(1)}, u32[]{:S(2)}, u32[]{:S(2)}) async-start(bf16[4,16,8,512]{3,2,0,1:T(8,128)(2,1)} %copy.20), calls=%async_computation.1 | async-start | bytes 1048576 | tf_op jit(solution)/shard_map/all_to_all | solution.py:131
  337.7 13.3 %all-to-all-done.1 = bf16[4,16,8,512]{3,2,0,1:T(8,128)(2,1)S(1)} async-done(((bf16[4,16,8,512]{3,2,0,1:T(8,128)(2,1)}), bf16[4,16,8,512]{3,2,0,1:T(8,128)(2,1)S(1)}, u32[]{:S(2)}, u32[]{:S(2)}) %all-to-all-start.1) | async-done | bytes 524320 | tf_op jit(solution)/shard_map/all_to_all | solution.py:131
  (264 shorter events, 130.5 us)
Async XLA Ops:
  0.0 159.8 %copy-start = (bf16[512,512]{1,0:T(8,128)(2,1)S(1)}, bf16[512,512]{1,0:T(8,128)(2,1)}, u32[]{:S(2)}) copy-start(bf16[512,512]{1,0:T(8,128)(2,1)} %param.26) | copy-start | bytes 1572868
  0.0 1.0 copy-start.2
  1.0 13.4 %copy-start.6 = (s32[64]{0:T(128)S(1)}, s32[64]{0:T(128)}, u32[]{:S(2)}) copy-start(s32[64]{0:T(128)} %param.29) | copy-start | bytes 772
  1.0 15.2 %copy-start.3 = (bf16[2048,128]{1,0:T(8,128)(2,1)S(1)}, bf16[2048,128]{1,0:T(8,128)(2,1)}, u32[]{:S(2)}) copy-start(bf16[2048,128]{1,0:T(8,128)(2,1)} %param.21) | copy-start | bytes 1572868
  23.2 118.8 %copy-start.4 = (bf16[512,512]{1,0:T(8,128)(2,1)S(1)}, bf16[512,512]{1,0:T(8,128)(2,1)}, u32[]{:S(2)}) copy-start(bf16[512,512]{1,0:T(8,128)(2,1)} %param.20) | copy-start | bytes 1572868
  23.2 118.8 %copy-start.5 = (bf16[512,512]{1,0:T(8,128)(2,1)S(1)}, bf16[512,512]{1,0:T(8,128)(2,1)}, u32[]{:S(2)}) copy-start(bf16[512,512]{1,0:T(8,128)(2,1)} %param.24) | copy-start | bytes 1572868
  23.2 119.3 %all-to-all-start = ((bf16[16,16,64,128]{3,2,1,0:T(8,128)(2,1)}), bf16[16,16,64,128]{3,2,1,0:T(8,128)(2,1)}, u32[]{:S(2)}, u32[]{:S(2)}) async-start(bf16[16,16,64,128]{3,2,1,0:T(8,128)(2,1)} %select_select_fusion), calls=%async_computation | async-start | bytes 8388608 | tf_op jit(solution)/shard_map/all_to_all | solution.py:69
  142.5 7.5 %copy-start.8 = (bf16[128,512]{1,0:T(8,128)(2,1)S(1)}, bf16[128,512]{1,0:T(8,128)(2,1)}, u32[]{:S(2)}) copy-start(bf16[128,512]{1,0:T(8,128)(2,1)} %param.22) | copy-start | bytes 393220
  142.5 7.5 %copy-start.9 = (f32[512]{0:T(512)S(1)}, f32[512]{0:T(512)}, u32[]{:S(2)}) copy-start(f32[512]{0:T(512)} %param.23) | copy-start | bytes 6148
  156.6 3.2 copy-start.11
  159.8 4.7 %copy-start.7 = (bf16[512,512]{1,0:T(8,128)(2,1)S(1)}, bf16[512,512]{1,0:T(8,128)(2,1)}, u32[]{:S(2)}) copy-start(bf16[512,512]{1,0:T(8,128)(2,1)} %param.25) | copy-start | bytes 1572868
  329.2 8.4 %copy-start.10 = (s32[64]{0:T(128)S(1)}, s32[64]{0:T(128)}, u32[]{:S(2)}) copy-start(s32[64]{0:T(128)} %param.31) | copy-start | bytes 772
  329.2 23.5 %copy-start.1 = (bf16[512,512]{1,0:T(8,128)(2,1)S(1)}, bf16[512,512]{1,0:T(8,128)(2,1)}, u32[]{:S(2)}) copy-start(bf16[512,512]{1,0:T(8,128)(2,1)} %param.26) | copy-start | bytes 1572868
  331.6 19.5 %all-to-all-start.1 = ((bf16[4,16,8,512]{3,2,0,1:T(8,128)(2,1)}), bf16[4,16,8,512]{3,2,0,1:T(8,128)(2,1)S(1)}, u32[]{:S(2)}, u32[]{:S(2)}) async-start(bf16[4,16,8,512]{3,2,0,1:T(8,128)(2,1)} %copy.20), calls=%async_computation.1 | async-start | bytes 1048576 | tf_op jit(solution)/shard_map/all_to_all | solution.py:131
where the time goes:
time: 358 us; the launch traced here: 353 us
  matrix products  116 us (32%)
  blocking collectives  108 us (30%)
  local copies, waits for them, and re-layouts  57.2 us (16%)
  other arithmetic  23 us (6%)
  loops' own time  21.6 us (6%)
  waiting for transfers between devices  13.4 us (4%)
  starting transfers between devices  12.6 us (4%)
    psum x1, blocking collectives, local(): lax.psum((jnp.sum(obs_wide, axis=0), jnp.sum(obs_wide * obs_wide, axis=0)...  108 us
    dot_general x32, matrix products, one_head(): lax.dot_general(query_head, key_head, (((1,), (1,)), ((), ())), preferred...  48.2 us
    dot_general x32, matrix products, one_head(): jnp.dot(weights_bf, value_head, preferred_element_type=jnp.float32) / totals  46.3 us
    another operation x4, loops' own time, local(): per_head = lax.map(one_head, jnp.arange(HEADS, dtype=jnp.int32))  21.6 us
    dynamic_slice x32, local copies, waits for them, and re-layouts, local(): per_head = lax.map(one_head, jnp.arange(HEADS, dtype=jnp.int32))  20 us
    all_to_all x1, waiting for transfers between devices, local(): lax.all_to_all(outgoing, 'tile', split_axis=1, concat_axis=0, tiled=True)  13.3 us
    gather x2, local copies, waits for them, and re-layouts, local(): spots = jnp.take(block_position, block_lists, axis=0)  13.3 us
    reduce_sum x32, other arithmetic, one_head(): totals = jnp.sum(expo, axis=-1, keepdims=True)  9.72 us
  transfers between devices with their start and end apart: 2, of which 1 were waited for; matrix products, arithmetic and copies ran while one was open for 1% of the time, Pallas kernels for 0%

commit v1 on v0

v1 whole, which is shorter than its diff:
```python
import functools

import jax
import jax.numpy as jnp
from jax import lax
from jax.experimental import pallas as pl
from jax.experimental.pallas import tpu as pltpu
from jax.sharding import PartitionSpec as P

HEADS = 8
BLOCK = 64
NSEL = 32
TILE_ROWS = 128
CHUNK = 512
NEG = -1e30


def attend_kernel(
    pick_ref,
    count_ref,
    grid_ref,
    blocks_ref,
    mean_ref,
    rstd_ref,
    w_obs_ref,
    b_obs_ref,
    w_query_ref,
    w_key_ref,
    w_value_ref,
    w_out_ref,
    out_ref,
    raw,
    keys,
    values,
    copy_sem,
):
    tile = pl.program_id(0)
    tiles = pl.num_programs(0)
    key_span = NSEL * BLOCK
    width = grid_ref.shape[1]
    pair = 2 * (width // HEADS)

    def fetch(which):
        slot = lax.rem(which, 2)

        def one(j, carry):
            spot = pick_ref[which * NSEL + j]
            pltpu.make_async_copy(
                blocks_ref.at[pl.ds(spot * BLOCK, BLOCK), :],
                raw.at[slot, pl.ds(j * BLOCK, BLOCK), :],
                copy_sem.at[slot],
            ).start()
            return carry

        lax.fori_loop(0, NSEL, one, 0)

    @pl.when(tile == 0)
    def _():
        fetch(tile)

    slot = lax.rem(tile, 2)
    pltpu.make_async_copy(
        blocks_ref.at[pl.ds(0, key_span), :], raw.at[slot], copy_sem.at[slot]
    ).wait()

    @pl.when(tile + 1 < tiles)
    def _():
        fetch(tile + 1)

    for start in range(0, key_span, CHUNK):
        rows = pl.ds(start, CHUNK)
        feats = raw[slot, rows, :].astype(jnp.float32)
        normed = ((feats - mean_ref[...]) * rstd_ref[...]).astype(jnp.bfloat16)
        hidden = jnp.dot(normed, w_obs_ref[...], preferred_element_type=jnp.float32)
        hidden = hidden + b_obs_ref[...]
        embedded = jax.nn.gelu(hidden, approximate=True).astype(jnp.bfloat16)
        keys[rows, :] = jnp.dot(
            embedded, w_key_ref[...], preferred_element_type=jnp.float32
        ).astype(jnp.bfloat16)
        values[rows, :] = jnp.dot(
            embedded, w_value_ref[...], preferred_element_type=jnp.float32
        ).astype(jnp.bfloat16)

    queries = jnp.dot(
        grid_ref[...], w_query_ref[...], preferred_element_type=jnp.float32
    ).astype(jnp.bfloat16)
    queries = queries * jnp.bfloat16(1.0 / (width // HEADS) ** 0.5)
    used = count_ref[tile] * BLOCK
    key_index = lax.broadcasted_iota(jnp.int32, (1, key_span), 1)
    bias = jnp.where(key_index < used, 0.0, NEG).astype(jnp.float32)
    lane = lax.broadcasted_iota(jnp.int32, (TILE_ROWS, pair), 1)
    first = lane < pair // 2
    zero = jnp.zeros((), jnp.bfloat16)
    parts = []
    for p in range(HEADS // 2):
        columns = slice(p * pair, (p + 1) * pair)
        q = queries[:, columns]
        both = jnp.concatenate([jnp.where(first, q, zero), jnp.where(first, zero, q)], axis=0)
        scores = lax.dot_general(
            both,
            keys[:, columns],
            (((1,), (1,)), ((), ())),
            preferred_element_type=jnp.float32,
        )
        scores = scores + bias
        peak = jnp.max(scores, axis=-1, keepdims=True)
        expo = jnp.exp(scores - peak)
        totals = jnp.sum(expo, axis=-1, keepdims=True)
        mixed = jnp.dot(
            expo.astype(jnp.bfloat16), values[:, columns], preferred_element_type=jnp.float32
        )
        mixed = mixed / totals
        parts.append(
            jnp.where(first, mixed[:TILE_ROWS], mixed[TILE_ROWS:]).astype(jnp.bfloat16)
        )
    attended = jnp.concatenate(parts, axis=1)
    out_ref[...] = jnp.dot(
        attended, w_out_ref[...], preferred_element_type=jnp.float32
    ).astype(jnp.bfloat16)


def attend(
    pick, counts, grid_tokens, blocks, mean, rstd, w_obs, b_obs, w_query, w_key, w_value, w_out
):
    rows, width = grid_tokens.shape
    feat = blocks.shape[1]
    key_span = NSEL * BLOCK

    def whole(shape):
        return pl.BlockSpec(shape, lambda t, *_: (0, 0))

    square = whole((width, width))
    return pl.pallas_call(
        attend_kernel,
        grid_spec=pltpu.PrefetchScalarGridSpec(
            num_scalar_prefetch=2,
            grid=(rows // TILE_ROWS,),
            in_specs=[
                pl.BlockSpec((TILE_ROWS, width), lambda t, *_: (t, 0)),
                pl.BlockSpec(memory_space=pl.ANY),
                whole((1, feat)),
                whole((1, feat)),
                whole((feat, width)),
                whole((1, width)),
                square,
                square,
                square,
                square,
            ],
            out_specs=pl.BlockSpec((TILE_ROWS, width), lambda t, *_: (t, 0)),
            scratch_shapes=[
                pltpu.VMEM((2, key_span, feat), jnp.bfloat16),
                pltpu.VMEM((key_span, width), jnp.bfloat16),
                pltpu.VMEM((key_span, width), jnp.bfloat16),
                pltpu.SemaphoreType.DMA((2,)),
            ],
        ),
        out_shape=jax.ShapeDtypeStruct((rows, width), jnp.bfloat16),
        compiler_params=pltpu.CompilerParams(dimension_semantics=("arbitrary",)),
        cost_estimate=pl.CostEstimate(
            flops=12_000_000_000, bytes_accessed=6_000_000, transcendentals=12_000_000
        ),
    )(
        pick,
        counts,
        grid_tokens,
        blocks,
        mean[None],
        rstd[None],
        w_obs,
        b_obs[None],
        w_query,
        w_key,
        w_value,
        w_out,
    )


def exchange(obs_features, block_lists, block_counts, block_position, tile_count, own_index):
    obs_blocks = obs_features.shape[0] // BLOCK
    tile_local = block_lists.shape[0] // tile_count
    entry_count = tile_local * NSEL
    capacity = max(2, 2 * entry_count // tile_count)
    spots = jnp.take(block_position, block_lists, axis=0)
    is_valid = jnp.arange(NSEL, dtype=jnp.int32)[None, :] < block_counts[:, None]
    owner_dev = (spots // obs_blocks).reshape(tile_count, entry_count)
    local_blk = (spots % obs_blocks).reshape(tile_count, entry_count)
    valid_rows = is_valid.reshape(tile_count, entry_count)
    entry_order = jnp.arange(entry_count, dtype=jnp.int32)
    earlier = (
        (owner_dev[:, :, None] == owner_dev[:, None, :])
        & valid_rows[:, None, :]
        & (entry_order[None, :] < entry_order[:, None])[None, :, :]
    )
    slot_rank = jnp.sum(earlier.astype(jnp.int32), axis=2)
    mine = valid_rows & (owner_dev == own_index)
    slot_ids = jnp.arange(capacity, dtype=jnp.int32)
    hits = mine[:, None, :] & (slot_rank[:, None, :] == slot_ids[None, :, None])
    slot_block = jnp.sum(jnp.where(hits, local_blk[:, None, :], 0), axis=2)
    my_owner = lax.dynamic_index_in_dim(owner_dev, own_index, 0, keepdims=False)
    my_rank = lax.dynamic_index_in_dim(slot_rank, own_index, 0, keepdims=False)
    my_valid = lax.dynamic_index_in_dim(valid_rows, own_index, 0, keepdims=False)
    pick = jnp.where(my_valid, my_owner * capacity + my_rank, 0)
    raw_blocks = obs_features.reshape(obs_blocks, BLOCK, obs_features.shape[1])
    incoming = lax.all_to_all(
        jnp.take(raw_blocks, slot_block, axis=0), "tile", split_axis=0, concat_axis=0, tiled=True
    )
    return incoming.reshape(tile_count * capacity * BLOCK, obs_features.shape[1]), pick


def local(
    grid_tokens,
    obs_features,
    w_obs,
    b_obs,
    w_query,
    w_key,
    w_value,
    w_out,
    block_lists,
    block_counts,
    block_position,
    proc_order,
):
    tile_count = lax.axis_size("tile")
    own_index = lax.axis_index("tile")
    tile_local = grid_tokens.shape[0] // TILE_ROWS
    width = grid_tokens.shape[1]
    obs_wide = obs_features.astype(jnp.float32)
    first_sum, second_sum = lax.psum(
        (jnp.sum(obs_wide, axis=0), jnp.sum(obs_wide * obs_wide, axis=0)), "tile"
    )
    obs_total = obs_features.shape[0] * tile_count
    feat_mean = first_sum / obs_total
    feat_rstd = lax.rsqrt(second_sum / obs_total - feat_mean * feat_mean + 1e-05)
    my_counts = lax.dynamic_slice_in_dim(block_counts, own_index * tile_local, tile_local)
    if tile_count <= 16:
        blocks = lax.all_gather(obs_features, "tile", axis=0, tiled=True)
        my_lists = lax.dynamic_slice_in_dim(block_lists, own_index * tile_local, tile_local)
        pick = jnp.take(block_position, my_lists.reshape(-1), axis=0)
    else:
        blocks, pick = exchange(
            obs_features, block_lists, block_counts, block_position, tile_count, own_index
        )
    encoded = attend(
        pick,
        my_counts,
        grid_tokens,
        blocks,
        feat_mean,
        feat_rstd,
        w_obs,
        b_obs,
        w_query,
        w_key,
        w_value,
        w_out,
    )
    outgoing = encoded.reshape(tile_local, tile_count, TILE_ROWS // tile_count, width)
    arrived = lax.all_to_all(outgoing, "tile", split_axis=1, concat_axis=0, tiled=True)
    arrived = arrived.reshape(tile_count * tile_local, TILE_ROWS // tile_count, width)
    return jnp.take(arrived, proc_order, axis=0).reshape(
        tile_count * tile_local * (TILE_ROWS // tile_count), width
    )


def solution(mesh):
    in_specs = (
        P(("groups", "tile"), None),
        P(("groups", "tile"), None),
        P(),
        P(),
        P(),
        P(),
        P(),
        P(),
        P("groups", None),
        P("groups"),
        P("groups"),
        P("groups"),
    )
    out_specs = P(("groups", "tile"), None)
    return jax.shard_map(local, mesh=mesh, in_specs=in_specs, out_specs=out_specs, check_vma=False)
```

time: 358 us -> 149 us (0.42)
  matrix products: 116 us -> 0 us
  blocking collectives: 108 us -> 24.2 us
  local copies, waits for them, and re-layouts: 57.2 us -> 5.88 us
  waiting for transfers between devices: 13.4 us -> 61.4 us
  Pallas kernels: 0 us -> 33.7 us
  loops' own time: 21.6 us -> 0 us
  other arithmetic: 23 us -> 3.39 us
  between operations: 0.45 us -> 13.5 us
  starting transfers between devices: 12.6 us -> 4.99 us
    dot_general x69 -> x0, matrix products: 116 us -> none  [the longest x32 48.2 us: one_head(): lax.dot_general(query_head, key_head, (((1,), (1,)), ((), ())), preferred...]
    psum x1, blocking collectives: 108 us -> 24.2 us  [local(): lax.psum((jnp.sum(obs_wide, axis=0), jnp.sum(obs_wide * obs_wide, axis=0)...]
    all_gather x0 -> x1, waiting for transfers between devices: none -> 47.3 us  [local(): blocks = lax.all_gather(obs_features, 'tile', axis=0, tiled=True)]
    pallas_call x0 -> x1, Pallas kernels: none -> 33.7 us  [attend(): pl.pallas_call(attend_kernel, grid_spec=pltpu.PrefetchScalarGridSpec(num_...]
    another operation x4 -> x0, loops' own time: 21.6 us -> none  [local(): per_head = lax.map(one_head, jnp.arange(HEADS, dtype=jnp.int32))]
    dynamic_slice x32 -> x2, local copies, waits for them, and re-layouts: 20 us -> 0.16 us  [local(): lax.dynamic_slice_in_dim(block_lists, own_index * tile_local, tile_local)]
    gather x4 -> x1, local copies, waits for them, and re-layouts: 19.5 us -> 1.64 us  [local(): pick = jnp.take(block_position, my_lists.reshape(-1), axis=0)]
    reduce_sum x35 -> x1, other arithmetic: 11 us -> 1.33 us  [local(): jnp.sum(obs_wide * obs_wide, axis=0)]
  transfers between devices with their start and end apart: 2 -> 2, of which waited for: 1 -> 2; matrix products, arithmetic and copies ran while one was open for 1% -> 4% of each run, Pallas kernels for 0% -> 0%
where the time goes in v1:
time: 149 us; the launch traced here: 147 us
  waiting for transfers between devices  61.4 us (41%)
  Pallas kernels  33.7 us (23%)
  blocking collectives  24.2 us (16%)
  between operations  13.5 us (9%)
  local copies, waits for them, and re-layouts  5.88 us (4%)
  starting transfers between devices  4.99 us (3%)
  other arithmetic  3.39 us (2%)
    all_gather x1, waiting for transfers between devices, local(): blocks = lax.all_gather(obs_features, 'tile', axis=0, tiled=True)  47.3 us
    pallas_call x1, Pallas kernels, attend(): pl.pallas_call(attend_kernel, grid_spec=pltpu.PrefetchScalarGridSpec(num_...  33.7 us
    psum x1, blocking collectives, local(): lax.psum((jnp.sum(obs_wide, axis=0), jnp.sum(obs_wide * obs_wide, axis=0)...  24.2 us
    all_to_all x1, waiting for transfers between devices, local(): lax.all_to_all(outgoing, 'tile', split_axis=1, concat_axis=0, tiled=True)  13.4 us
    all_to_all x1, starting transfers between devices, local(): lax.all_to_all(outgoing, 'tile', split_axis=1, concat_axis=0, tiled=True)  4.99 us
  transfers between devices with their start and end apart: 2, of which 2 were waited for; matrix products, arithmetic and copies ran while one was open for 4% of the time, Pallas kernels for 0%

profile of v1, /device:TPU:13, one launch (start us, length us, event | category | flops | bytes accessed | tf_op | source)
XLA Modules:
  0.0 147.0 jit_solution(17586539136502712147)
XLA Ops:
  6.5 0.0 copy-start
  6.5 0.0 all-gather.2.cloned.1.call-start
  6.5 0.7 all-gather.2.cloned.1.call-update
  7.3 0.0 copy-done
  7.3 0.1 constant_dynamic-slice_fusion
  7.4 0.1 copy.15
  7.4 0.1 reshape.55
  7.5 0.1 reshape.54
  7.6 1.3 dynamic_slice.7.count_ref
  8.9 1.6 %gather_fusion = s32[128]{0:T(128)S(1)} fusion(s32[512]{0:T(512)} %param.22, s32[1024]{0:T(1024)S(1)} %pad_clamp_fusion.1), kind=kCustom, calls=%fused_computation | custom fusion | bytes 1536 | tf_op jit(solution)/shard_map/jit(_take)/gather | solution.py:240
  10.5 1.3 fusion
  11.8 24.2 %all-reduce = (f32[128]{0:T(128)S(1)}, f32[128]{0:T(128)S(1)}) all-reduce(f32[128]{0:T(128)S(1)} %get-tuple-element.6, f32[128]{0:T(128)S(1)} %get-tuple-element.5), channel_id=1, replica_groups=mesh['groups'=2,'tile'=16] {'tile'}, use_global_device_ids=true, to_apply=%region_1.0 | all-reduce | flops 256 | bytes 2048 | tf_op jit(solution)/shard_map/psum | solution.py:230
  36.1 0.5 and_select_fusion.pick_ref
  36.6 0.6 rsqrt_bitcast_fusion
  37.2 47.3 %all-gather.2.cloned.1.call-done.blocks_ref = bf16[32768,128]{1,0:T(8,128)(2,1)} async-done(((bf16[2048,128]{1,0:T(8,128)(2,1)}), bf16[32768,128]{1,0:T(8,128)(2,1)}) %all-gather.2.cloned.1.call-update) | async-done | bytes 8388624 | tf_op jit(solution)/shard_map/all_gather | solution.py:238
  84.4 33.7 %shard_map.118 = bf16[512,512]{1,0:T(8,128)(2,1)} custom-call(s32[128]{0:T(128)} %and_select_fusion.pick_ref, s32[4]{0:T(128)} %dynamic_slice.7.count_ref, bf16[512,512]{1,0:T(8,128)(2,1)} %grid_ref.1, bf16[32768,128]{1,0:T(8,128)(2,1)} %all-gather.2.cloned.1.call-done.blocks_ref, f32[1,128]{1,0:T(1,128)} %get-tuple-element.10.mean_ref, ...), custom_call_target="tpu_custom_call" | custom-call | flops 12000000000 | bytes 6000000 | tf_op jit(solution)/shard_map/pallas_call | solution.py:133
  118.1 1.9 %copy.17 = bf16[4,16,8,512]{3,2,0,1:T(8,128)(2,1)} copy(bf16[4,16,8,512]{3,2,1,0:T(8,128)(2,1)} %bitcast.16) | data formatting | bytes 1048576 | tf_op jit(solution)/shard_map/reshape | solution.py:259
  120.0 5.0 %all-to-all-start = ((bf16[4,16,8,512]{3,2,0,1:T(8,128)(2,1)}), bf16[4,16,8,512]{3,2,0,1:T(8,128)(2,1)S(1)}, u32[]{:S(2)}, u32[]{:S(2)}) async-start(bf16[4,16,8,512]{3,2,0,1:T(8,128)(2,1)} %copy.17), calls=%async_computation | async-start | bytes 1048576 | tf_op jit(solution)/shard_map/all_to_all | solution.py:260
  125.0 0.0 copy-done.1
  125.0 0.1 broadcast_in_dim.31
  125.1 0.1 broadcast_in_dim.32
  125.2 13.4 %all-to-all-done = bf16[4,16,8,512]{3,2,0,1:T(8,128)(2,1)S(1)} async-done(((bf16[4,16,8,512]{3,2,0,1:T(8,128)(2,1)}), bf16[4,16,8,512]{3,2,0,1:T(8,128)(2,1)S(1)}, u32[]{:S(2)}, u32[]{:S(2)}) %all-to-all-start) | async-done | bytes 524320 | tf_op jit(solution)/shard_map/all_to_all | solution.py:260
  138.6 0.6 gather_fusion.1
  139.2 0.9 bitcast_select_fusion
  (6 shorter events, 0.0 us)
Async XLA Ops:
  6.5 0.7 copy-start
  6.5 77.9 %all-gather.2.cloned.1.call-start = ((), (), s32[]{:S(2)}) async-start(), calls=%async_computation.1 | async-start | bytes 8912896 | tf_op jit(solution)/shard_map/all_gather | solution.py:238
  84.4 40.5 %copy-start.1 = (s32[64]{0:T(128)S(1)}, s32[64]{0:T(128)}, u32[]{:S(2)}) copy-start(s32[64]{0:T(128)} %param.23) | copy-start | bytes 772
  120.0 18.6 %all-to-all-start = ((bf16[4,16,8,512]{3,2,0,1:T(8,128)(2,1)}), bf16[4,16,8,512]{3,2,0,1:T(8,128)(2,1)S(1)}, u32[]{:S(2)}, u32[]{:S(2)}) async-start(bf16[4,16,8,512]{3,2,0,1:T(8,128)(2,1)} %copy.17), calls=%async_computation | async-start | bytes 1048576 | tf_op jit(solution)/shard_map/all_to_all | solution.py:260
Sparse Core Ops, SparseCore 0:
  9.5 74.8 all-gather.1

commit v2 on v1

--- a/solution.py
+++ b/solution.py
@@ -114,15 +114,29 @@
             jnp.where(first, mixed[:TILE_ROWS], mixed[TILE_ROWS:]).astype(jnp.bfloat16)
         )
     attended = jnp.concatenate(parts, axis=1)
-    out_ref[...] = jnp.dot(
+    encoded = jnp.dot(
         attended, w_out_ref[...], preferred_element_type=jnp.float32
     ).astype(jnp.bfloat16)
+    out_ref[...] = encoded.reshape(out_ref.shape)
 
 
 def attend(
-    pick, counts, grid_tokens, blocks, mean, rstd, w_obs, b_obs, w_query, w_key, w_value, w_out
+    tile_count,
+    pick,
+    counts,
+    grid_tokens,
+    blocks,
+    mean,
+    rstd,
+    w_obs,
+    b_obs,
+    w_query,
+    w_key,
+    w_value,
+    w_out,
 ):
     rows, width = grid_tokens.shape
+    piece = TILE_ROWS // tile_count
     feat = blocks.shape[1]
     key_span = NSEL * BLOCK
 
@@ -147,7 +161,7 @@
                 square,
                 square,
             ],
-            out_specs=pl.BlockSpec((TILE_ROWS, width), lambda t, *_: (t, 0)),
+            out_specs=pl.BlockSpec((tile_count, 1, piece, width), lambda t, *_: (0, t, 0, 0)),
             scratch_shapes=[
                 pltpu.VMEM((2, key_span, feat), jnp.bfloat16),
                 pltpu.VMEM((key_span, width), jnp.bfloat16),
@@ -155,7 +169,9 @@
                 pltpu.SemaphoreType.DMA((2,)),
             ],
         ),
-        out_shape=jax.ShapeDtypeStruct((rows, width), jnp.bfloat16),
+        out_shape=jax.ShapeDtypeStruct(
+            (tile_count, rows // TILE_ROWS, piece, width), jnp.bfloat16
+        ),
         compiler_params=pltpu.CompilerParams(dimension_semantics=("arbitrary",)),
         cost_estimate=pl.CostEstimate(
             flops=12_000_000_000, bytes_accessed=6_000_000, transcendentals=12_000_000
@@ -165,8 +181,8 @@
         counts,
         grid_tokens,
         blocks,
-        mean[None],
-        rstd[None],
+        mean,
+        rstd,
         w_obs,
         b_obs[None],
         w_query,
@@ -174,6 +190,240 @@
         w_value,
         w_out,
     )
+
+
+MESH = pl.DeviceIdType.MESH
+
+
+def greet_all(me, count):
+    barrier = pltpu.get_barrier_semaphore()
+
+    def one(k, carry):
+        peer = lax.rem(me + k, count)
+        pl.semaphore_signal(barrier, inc=1, device_id={"tile": peer}, device_id_type=MESH)
+        return carry
+
+    lax.fori_loop(1, count, one, 0)
+    pl.semaphore_wait(barrier, count - 1)
+
+
+def gather_kernel(
+    lines, obs_ref, all_ref, mean_ref, rstd_ref, part, parts, sends, recvs, part_sends, part_recvs, own_sem
+):
+    count = 4 * lines
+    me = lax.axis_index("tile")
+    z, y, c = me // 4, lax.rem(me // 2, 2), lax.rem(me, 2)
+    rows = obs_ref.shape[0]
+
+    def index(zz, yy, cc):
+        return (zz * 2 + yy) * 2 + cc
+
+    def place(block):
+        return all_ref.at[pl.ds(pl.multiple_of(block * rows, rows), rows), :]
+
+    def send(source, block, way, target):
+        return pltpu.make_async_remote_copy(
+            src_ref=source,
+            dst_ref=place(block),
+            send_sem=sends.at[way, block],
+            recv_sem=recvs.at[block],
+            device_id={"tile": target},
+            device_id_type=MESH,
+        )
+
+    down, up = index(z - 1, y, c), index(z + 1, y, c)
+    across, beside = index(z, 1 - y, c), index(z, y, 1 - c)
+
+    greet_all(me, count)
+    own = pltpu.make_async_copy(obs_ref, place(me), own_sem)
+
+    @pl.when(z > 0)
+    def _():
+        send(obs_ref, me, 0, down).start()
+
+    @pl.when(z < lines - 1)
+    def _():
+        send(obs_ref, me, 1, up).start()
+
+    send(obs_ref, me, 2, across).start()
+    send(obs_ref, me, 3, beside).start()
+    own.start()
+
+    feats = obs_ref[...].astype(jnp.float32)
+    part[...] = jnp.zeros_like(part)
+    part[0:1, :] = jnp.sum(feats, axis=0, keepdims=True)
+    part[1:2, :] = jnp.sum(feats * feats, axis=0, keepdims=True)
+    parts[pl.ds(me, 1)] = part[...][None]
+
+    for hop in range(1, lines + 1):
+        if hop < lines:
+            from_up, from_down = index(z + hop, y, c), index(z - hop, y, c)
+
+            @pl.when(z + hop < lines)
+            def _():
+                send(place(from_up), from_up, 3, beside).wait_recv()
+
+                @pl.when(z > 0)
+                def _():
+                    send(place(from_up), from_up, 0, down).start()
+
+                send(place(from_up), from_up, 2, across).start()
+                send(place(from_up), from_up, 3, beside).start()
+
+            @pl.when(z - hop >= 0)
+            def _():
+                send(place(from_down), from_down, 3, beside).wait_recv()
+
+                @pl.when(z < lines - 1)
+                def _():
+                    send(place(from_down), from_down, 1, up).start()
+
+                send(place(from_down), from_down, 2, across).start()
+                send(place(from_down), from_down, 3, beside).start()
+
+        if hop == 1:
+
+            def share(k, carry):
+                peer = lax.rem(me + k, count)
+                pltpu.make_async_remote_copy(
+                    src_ref=part,
+                    dst_ref=parts.at[me],
+                    send_sem=part_sends.at[k],
+                    recv_sem=part_recvs.at[me],
+                    device_id={"tile": peer},
+                    device_id_type=MESH,
+                ).start()
+                return carry
+
+            lax.fori_loop(1, count, share, 0)
+
+        far = hop - 1
+        for sign in (1, -1) if far else (1,):
+            other = index(z + sign * far, 1 - y, c)
+
+            @pl.when((z + sign * far >= 0) & (z + sign * far < lines))
+            def _():
+                send(place(other), other, 3, beside).wait_recv()
+                send(place(other), other, 3, beside).start()
+
+    def gathered(k, carry):
+        peer = lax.rem(me + k, count)
+        copy = pltpu.make_async_remote_copy(
+            src_ref=part,
+            dst_ref=parts.at[peer],
+            send_sem=part_sends.at[k],
+            recv_sem=part_recvs.at[peer],
+            device_id={"tile": peer},
+            device_id_type=MESH,
+        )
+        copy.wait_send()
+        copy.wait_recv()
+        return carry
+
+    lax.fori_loop(1, count, gathered, 0)
+    sums = jnp.sum(parts[...], axis=0)
+    total = rows * count
+    mean = sums[0:1, :] / total
+    mean_ref[...] = mean
+    rstd_ref[...] = lax.rsqrt(sums[1:2, :] / total - mean * mean + 1e-05)
+
+    for zz in range(lines):
+        for yy in range(2):
+            theirs, mine = index(zz, yy, 1 - c), index(zz, yy, c)
+            send(place(theirs), theirs, 3, beside).wait_recv()
+            send(place(mine), mine, 3, beside).wait_send()
+        held = index(zz, y, c)
+        send(place(held), held, 2, across).wait_send()
+
+        @pl.when((zz >= z) & (z > 0))
+        def _():
+            send(place(held), held, 0, down).wait_send()
+
+        @pl.when((zz <= z) & (z < lines - 1))
+        def _():
+            send(place(held), held, 1, up).wait_send()
+
+    own.wait()
+
+
+def gather_blocks(obs_features, tile_count):
+    rows, feat = obs_features.shape
+    small = jax.ShapeDtypeStruct((1, feat), jnp.float32)
+    vmem = pl.BlockSpec(memory_space=pltpu.VMEM)
+    return pl.pallas_call(
+        functools.partial(gather_kernel, tile_count // 4),
+        out_shape=(
+            jax.ShapeDtypeStruct((tile_count * rows, feat), obs_features.dtype),
+            small,
+            small,
+        ),
+        in_specs=[vmem],
+        out_specs=(pl.BlockSpec(memory_space=pl.ANY), vmem, vmem),
+        scratch_shapes=[
+            pltpu.VMEM((8, feat), jnp.float32),
+            pltpu.VMEM((tile_count, 8, feat), jnp.float32),
+            pltpu.SemaphoreType.DMA((4, tile_count)),
+            pltpu.SemaphoreType.DMA((tile_count,)),
+            pltpu.SemaphoreType.DMA((tile_count,)),
+            pltpu.SemaphoreType.DMA((tile_count,)),
+            pltpu.SemaphoreType.DMA,
+        ],
+        compiler_params=pltpu.CompilerParams(collective_id=0, has_side_effects=True),
+    )(obs_features)
+
+
+def scatter_kernel(count, order_ref, encoded_ref, out_ref, arrived, sends, recvs):
+    me = lax.axis_index("tile")
+    tile_local = encoded_ref.shape[1]
+    greet_all(me, count)
+
+    def copy(source, peer, k):
+        return pltpu.make_async_remote_copy(
+            src_ref=encoded_ref.at[peer],
+            dst_ref=arrived.at[pl.ds(source * tile_local, tile_local)],
+            send_sem=sends.at[k],
+            recv_sem=recvs.at[source],
+            device_id={"tile": peer},
+            device_id_type=MESH,
+        )
+
+    def start(k, carry):
+        copy(me, lax.rem(me + k, count), k).start()
+        return carry
+
+    def finish(k, carry):
+        peer = lax.rem(me + k, count)
+        copy(peer, peer, k).wait_send()
+        copy(peer, peer, k).wait_recv()
+        return carry
+
+    lax.fori_loop(1, count, start, 0)
+    arrived[pl.ds(me * tile_local, tile_local)] = encoded_ref[me]
+    lax.fori_loop(1, count, finish, 0)
+
+    def arrange(j, carry):
+        out_ref[pl.ds(j, 1)] = arrived[pl.ds(order_ref[j], 1)]
+        return carry
+
+    lax.fori_loop(0, count * tile_local, arrange, 0, unroll=8)
+
+
+def scatter(encoded, proc_order):
+    count, tile_local, piece, width = encoded.shape
+    vmem = pl.BlockSpec(memory_space=pltpu.VMEM)
+    shape = (count * tile_local, piece, width)
+    return pl.pallas_call(
+        functools.partial(scatter_kernel, count),
+        out_shape=jax.ShapeDtypeStruct(shape, encoded.dtype),
+        in_specs=[pl.BlockSpec(memory_space=pltpu.SMEM), vmem],
+        out_specs=vmem,
+        scratch_shapes=[
+            pltpu.VMEM(shape, encoded.dtype),
+            pltpu.SemaphoreType.DMA((count,)),
+            pltpu.SemaphoreType.DMA((count,)),
+        ],
+        compiler_params=pltpu.CompilerParams(collective_id=1, has_side_effects=True),
+    )(proc_order, encoded).reshape(count * tile_local * piece, width)
 
 
 def exchange(obs_features, block_lists, block_counts, block_position, tile_count, own_index):
@@ -226,23 +476,29 @@
     own_index = lax.axis_index("tile")
     tile_local = grid_tokens.shape[0] // TILE_ROWS
     width = grid_tokens.shape[1]
-    obs_wide = obs_features.astype(jnp.float32)
-    first_sum, second_sum = lax.psum(
-        (jnp.sum(obs_wide, axis=0), jnp.sum(obs_wide * obs_wide, axis=0)), "tile"
-    )
-    obs_total = obs_features.shape[0] * tile_count
-    feat_mean = first_sum / obs_total
-    feat_rstd = lax.rsqrt(second_sum / obs_total - feat_mean * feat_mean + 1e-05)
     my_counts = lax.dynamic_slice_in_dim(block_counts, own_index * tile_local, tile_local)
-    if tile_count <= 16:
-        blocks = lax.all_gather(obs_features, "tile", axis=0, tiled=True)
+    near = tile_count <= 16 and tile_count % 4 == 0
+    if near:
+        blocks, feat_mean, feat_rstd = gather_blocks(obs_features, tile_count)
         my_lists = lax.dynamic_slice_in_dim(block_lists, own_index * tile_local, tile_local)
         pick = jnp.take(block_position, my_lists.reshape(-1), axis=0)
     else:
+        obs_wide = obs_features.astype(jnp.float32)
+        first_sum, second_sum = lax.psum(
+            (
+                jnp.sum(obs_wide, axis=0, keepdims=True),
+                jnp.sum(obs_wide * obs_wide, axis=0, keepdims=True),
+            ),
+            "tile",
+        )
+        obs_total = obs_features.shape[0] * tile_count
+        feat_mean = first_sum / obs_total
+        feat_rstd = lax.rsqrt(second_sum / obs_total - feat_mean * feat_mean + 1e-05)
         blocks, pick = exchange(
             obs_features, block_lists, block_counts, block_position, tile_count, own_index
         )
     encoded = attend(
+        tile_count if near else 1,
         pick,
         my_counts,
         grid_tokens,
@@ -256,6 +512,8 @@
         w_value,
         w_out,
     )
+    if near:
+        return scatter(encoded, proc_order)
     outgoing = encoded.reshape(tile_local, tile_count, TILE_ROWS // tile_count, width)
     arrived = lax.all_to_all(outgoing, "tile", split_axis=1, concat_axis=0, tiled=True)
     arrived = arrived.reshape(tile_count * tile_local, TILE_ROWS // tile_count, width)

time: 149 us -> 117 us (0.79)
  Pallas kernels: 33.7 us -> 111 us
  waiting for transfers between devices: 61.4 us -> 0 us
  blocking collectives: 24.2 us -> 0 us
  between operations: 13.5 us -> 0.04 us
  starting transfers between devices: 4.99 us -> 0 us
  other arithmetic: 3.39 us -> 0.54 us
    pallas_call x0 -> x2, Pallas kernels: none -> 77.2 us  [the longest x1 57.1 us: gather_blocks(): pl.pallas_call(functools.partial(gather_kernel, tile_count // 4), out_sha...]
    all_gather x1 -> x0, waiting for transfers between devices: 47.3 us -> none  [local(): blocks = lax.all_gather(obs_features, 'tile', axis=0, tiled=True)]
    psum x1 -> x0, blocking collectives: 24.2 us -> none  [local(): lax.psum((jnp.sum(obs_wide, axis=0), jnp.sum(obs_wide * obs_wide, axis=0)...]
    all_to_all x1 -> x0, waiting for transfers between devices: 13.4 us -> none  [local(): lax.all_to_all(outgoing, 'tile', split_axis=1, concat_axis=0, tiled=True)]
    all_to_all x1 -> x0, starting transfers between devices: 4.99 us -> none  [local(): lax.all_to_all(outgoing, 'tile', split_axis=1, concat_axis=0, tiled=True)]
    reshape x1 -> x0, local copies, waits for them, and re-layouts: 1.88 us -> none  [local(): encoded.reshape(tile_local, tile_count, TILE_ROWS // tile_count, width)]
    unnamed x4 -> x3, local copies, waits for them, and re-layouts: 0.01 us -> 1.87 us
  transfers between devices with their start and end apart: 2 -> 0, of which waited for: 2 -> 0; matrix products, arithmetic and copies ran while one was open for 4% -> 0% of each run, Pallas kernels for 0% -> 0%
where the time goes in v2:
time: 117 us; the launch traced here: 116 us
  Pallas kernels  111 us (95%)
  local copies, waits for them, and re-layouts  5.1 us (4%)
    pallas_call x1, Pallas kernels, gather_blocks(): pl.pallas_call(functools.partial(gather_kernel, tile_count // 4), out_sha...  57.1 us
    pallas_call x1, Pallas kernels, attend(): pl.pallas_call(attend_kernel, grid_spec=pltpu.PrefetchScalarGridSpec(num_...  33.5 us
    pallas_call x1, Pallas kernels, scatter(): pl.pallas_call(functools.partial(scatter_kernel, count), out_shape=jax.Sh...  20 us

profile of v2, /device:TPU:13, one launch (start us, length us, event | category | flops | bytes accessed | tf_op | source)
XLA Modules:
  0.0 116.4 jit_solution(8775826134221729462)
XLA Ops:
  0.0 0.0 copy-start
  0.0 1.3 %dynamic_slice.7.count_ref = s32[4]{0:T(128)} dynamic-slice(s32[64]{0:T(128)} %param.21, s32[]{:T(128)S(6)} %select_n.24), dynamic_slice_sizes={4} | dynamic-slice | bytes 36 | tf_op jit(solution)/shard_map/dynamic_slice | solution.py:479
  1.3 0.0 copy-done
  1.3 0.1 constant_dynamic-slice_fusion
  1.3 0.1 copy.15
  1.4 0.1 reshape.43
  1.5 0.1 reshape.42
  1.6 1.6 %gather_fusion = s32[128]{0:T(128)S(1)} fusion(s32[512]{0:T(512)} %param.22, s32[1024]{0:T(1024)S(1)} %pad_clamp_fusion), kind=kCustom, calls=%fused_computation | custom fusion | bytes 1536 | tf_op jit(solution)/shard_map/jit(_take)/gather | solution.py:484
  3.3 0.5 and_select_fusion.pick_ref
  3.8 57.1 %shard_map.118 = (bf16[32768,128]{1,0:T(8,128)(2,1)}, f32[1,128]{1,0:T(1,128)}, f32[1,128]{1,0:T(1,128)}) custom-call(bf16[2048,128]{1,0:T(8,128)(2,1)} %obs_ref.1), custom_call_target="tpu_custom_call" | custom-call | tf_op jit(solution)/shard_map/pallas_call | solution.py:353
  60.9 33.5 %shard_map.119.encoded_ref = bf16[16,4,8,512]{3,2,1,0:T(8,128)(2,1)} custom-call(s32[128]{0:T(128)} %and_select_fusion.pick_ref, s32[4]{0:T(128)} %dynamic_slice.7.count_ref, bf16[512,512]{1,0:T(8,128)(2,1)} %grid_ref.1, bf16[32768,128]{1,0:T(8,128)(2,1)} %get-tuple-element.8.blocks_ref, f32[1,128]{1,0:T(1,128)} %get-tuple-element.9.mean_ref, ...), custom_call_target="tpu_custom_call" | custom-call | flops 12000000000 | bytes 6000000 | tf_op jit(solution)/shard_map/pallas_call | solution.py:147
  94.5 20.0 %shard_map.120 = bf16[64,8,512]{2,1,0:T(8,128)(2,1)} custom-call(s32[64]{0:T(128)} %order_ref.1, bf16[16,4,8,512]{3,2,1,0:T(8,128)(2,1)} %shard_map.119.encoded_ref), custom_call_target="tpu_custom_call" | custom-call | tf_op jit(solution)/shard_map/pallas_call | solution.py:415
  114.5 1.9 %copy.18 = bf16[512,512]{1,0:T(8,128)(2,1)} copy(bf16[512,512]{1,0:T(8,128)(2,1)} %bitcast.4) | data formatting | bytes 1048576
  (2 shorter events, 0.0 us)
Async XLA Ops:
  0.0 1.3 %copy-start = (s32[64,32]{0,1:T(8,128)S(1)}, s32[64,32]{0,1:T(8,128)}, u32[]{:S(2)}) copy-start(s32[64,32]{0,1:T(8,128)} %param.20) | copy-start | bytes 24580

commit v3 on v2

--- a/solution.py
+++ b/solution.py
@@ -16,8 +16,10 @@
 
 
 def attend_kernel(
-    pick_ref,
+    owned,
+    list_ref,
     count_ref,
+    position_ref,
     grid_ref,
     blocks_ref,
     mean_ref,
@@ -39,12 +41,13 @@
     key_span = NSEL * BLOCK
     width = grid_ref.shape[1]
     pair = 2 * (width // HEADS)
+    base = lax.axis_index("tile") * tiles if owned else 0
 
     def fetch(which):
         slot = lax.rem(which, 2)
 
         def one(j, carry):
-            spot = pick_ref[which * NSEL + j]
+            spot = position_ref[list_ref[base + which, j]]
             pltpu.make_async_copy(
                 blocks_ref.at[pl.ds(spot * BLOCK, BLOCK), :],
                 raw.at[slot, pl.ds(j * BLOCK, BLOCK), :],
@@ -85,8 +88,9 @@
         grid_ref[...], w_query_ref[...], preferred_element_type=jnp.float32
     ).astype(jnp.bfloat16)
     queries = queries * jnp.bfloat16(1.0 / (width // HEADS) ** 0.5)
-    used = count_ref[tile] * BLOCK
-    key_index = lax.broadcasted_iota(jnp.int32, (1, key_span), 1)
+    certain = 3 * key_span // 4
+    used = count_ref[base + tile] * BLOCK
+    key_index = certain + lax.broadcasted_iota(jnp.int32, (1, key_span - certain), 1)
     bias = jnp.where(key_index < used, 0.0, NEG).astype(jnp.float32)
     lane = lax.broadcasted_iota(jnp.int32, (TILE_ROWS, pair), 1)
     first = lane < pair // 2
@@ -102,7 +106,7 @@
             (((1,), (1,)), ((), ())),
             preferred_element_type=jnp.float32,
         )
-        scores = scores + bias
+        scores = jnp.concatenate([scores[:, :certain], scores[:, certain:] + bias], axis=1)
         peak = jnp.max(scores, axis=-1, keepdims=True)
         expo = jnp.exp(scores - peak)
         totals = jnp.sum(expo, axis=-1, keepdims=True)
@@ -122,8 +126,10 @@
 
 def attend(
     tile_count,
-    pick,
+    owned,
+    lists,
     counts,
+    position,
     grid_tokens,
     blocks,
     mean,
@@ -145,9 +151,9 @@
 
     square = whole((width, width))
     return pl.pallas_call(
-        attend_kernel,
+        functools.partial(attend_kernel, owned),
         grid_spec=pltpu.PrefetchScalarGridSpec(
-            num_scalar_prefetch=2,
+            num_scalar_prefetch=3,
             grid=(rows // TILE_ROWS,),
             in_specs=[
                 pl.BlockSpec((TILE_ROWS, width), lambda t, *_: (t, 0)),
@@ -177,8 +183,9 @@
             flops=12_000_000_000, bytes_accessed=6_000_000, transcendentals=12_000_000
         ),
     )(
-        pick,
+        lists,
         counts,
+        position,
         grid_tokens,
         blocks,
         mean,
@@ -214,39 +221,47 @@
     me = lax.axis_index("tile")
     z, y, c = me // 4, lax.rem(me // 2, 2), lax.rem(me, 2)
     rows = obs_ref.shape[0]
+    half = rows // 2
+    odd = lax.rem(z, 2)
 
     def index(zz, yy, cc):
         return (zz * 2 + yy) * 2 + cc
 
-    def place(block):
-        return all_ref.at[pl.ds(pl.multiple_of(block * rows, rows), rows), :]
-
-    def send(source, block, way, target):
-        return pltpu.make_async_remote_copy(
-            src_ref=source,
-            dst_ref=place(block),
-            send_sem=sends.at[way, block],
-            recv_sem=recvs.at[block],
-            device_id={"tile": target},
-            device_id_type=MESH,
-        )
-
     down, up = index(z - 1, y, c), index(z + 1, y, c)
     across, beside = index(z, 1 - y, c), index(z, y, 1 - c)
+    buddy_z = z + 1 - 2 * odd
+    buddy = index(buddy_z, y, c)
+    targets = (down, up, across, beside, buddy)
+
+    def place(block, h):
+        return all_ref.at[pl.ds(pl.multiple_of(block * rows + h * half, half), half), :]
+
+    def send(block, h, way, own=False):
+        return pltpu.make_async_remote_copy(
+            src_ref=obs_ref.at[pl.ds(h * half, half), :] if own else place(block, h),
+            dst_ref=place(block, h),
+            send_sem=sends.at[way, 2 * block + h],
+            recv_sem=recvs.at[2 * block + h],
+            device_id={"tile": targets[way]},
+            device_id_type=MESH,
+        )
 
     greet_all(me, count)
-    own = pltpu.make_async_copy(obs_ref, place(me), own_sem)
-
-    @pl.when(z > 0)
-    def _():
-        send(obs_ref, me, 0, down).start()
-
-    @pl.when(z < lines - 1)
-    def _():
-        send(obs_ref, me, 1, up).start()
-
-    send(obs_ref, me, 2, across).start()
-    send(obs_ref, me, 3, beside).start()
+    for h in range(2):
+
+        @pl.when(z > 0)
+        def _():
+            send(me, h, 0, True).start()
+
+        @pl.when(z < lines - 1)
+        def _():
+            send(me, h, 1, True).start()
+
+        send(me, h, 2, True).start()
+        send(me, h, 3, True).start()
+    own = pltpu.make_async_copy(
+        obs_ref, all_ref.at[pl.ds(pl.multiple_of(me * rows, rows), rows), :], own_sem
+    )
     own.start()
 
     feats = obs_ref[...].astype(jnp.float32)
@@ -256,30 +271,56 @@
     parts[pl.ds(me, 1)] = part[...][None]
 
     for hop in range(1, lines + 1):
-        if hop < lines:
-            from_up, from_down = index(z + hop, y, c), index(z - hop, y, c)
-
-            @pl.when(z + hop < lines)
-            def _():
-                send(place(from_up), from_up, 3, beside).wait_recv()
-
-                @pl.when(z > 0)
+        for h in range(2):
+            if hop < lines:
+                from_up, from_down = index(z + hop, y, c), index(z - hop, y, c)
+
+                @pl.when(z + hop < lines)
                 def _():
-                    send(place(from_up), from_up, 0, down).start()
-
-                send(place(from_up), from_up, 2, across).start()
-                send(place(from_up), from_up, 3, beside).start()
-
-            @pl.when(z - hop >= 0)
-            def _():
-                send(place(from_down), from_down, 3, beside).wait_recv()
-
-                @pl.when(z < lines - 1)
+                    send(from_up, h, 3).wait_recv()
+
+                    @pl.when(z > 0)
+                    def _():
+                        send(from_up, h, 0).start()
+
+                    if hop == 1 and h == 1:
+
+                        @pl.when(odd == 1)
+                        def _():
+                            send(from_up, h, 2).start()
+
+                    else:
+                        send(from_up, h, 2).start()
+                    send(from_up, h, 3).start()
+
+                @pl.when(z - hop >= 0)
                 def _():
-                    send(place(from_down), from_down, 1, up).start()
-
-                send(place(from_down), from_down, 2, across).start()
-                send(place(from_down), from_down, 3, beside).start()
+                    send(from_down, h, 3).wait_recv()
+
+                    @pl.when(z < lines - 1)
+                    def _():
+                        send(from_down, h, 1).start()
+
+                    if hop == 1 and h == 1:
+
+                        @pl.when(odd == 0)
+                        def _():
+                            send(from_down, h, 2).start()
+
+                    else:
+                        send(from_down, h, 2).start()
+                    send(from_down, h, 3).start()
+
+            far = hop - 1
+            for sign in (1, -1) if far else (1,):
+                other = index(z + sign * far, 1 - y, c)
+
+                @pl.when((z + sign * far >= 0) & (z + sign * far < lines))
+                def _():
+                    send(other, h, 3).wait_recv()
+                    if far == 0 and h == 1:
+                        send(other, h, 4).start()
+                    send(other, h, 3).start()
 
         if hop == 1:
 
@@ -297,15 +338,6 @@
 
             lax.fori_loop(1, count, share, 0)
 
-        far = hop - 1
-        for sign in (1, -1) if far else (1,):
-            other = index(z + sign * far, 1 - y, c)
-
-            @pl.when((z + sign * far >= 0) & (z + sign * far < lines))
-            def _():
-                send(place(other), other, 3, beside).wait_recv()
-                send(place(other), other, 3, beside).start()
-
     def gathered(k, carry):
         peer = lax.rem(me + k, count)
         copy = pltpu.make_async_remote_copy(
@@ -328,21 +360,29 @@
     rstd_ref[...] = lax.rsqrt(sums[1:2, :] / total - mean * mean + 1e-05)
 
     for zz in range(lines):
-        for yy in range(2):
-            theirs, mine = index(zz, yy, 1 - c), index(zz, yy, c)
-            send(place(theirs), theirs, 3, beside).wait_recv()
-            send(place(mine), mine, 3, beside).wait_send()
         held = index(zz, y, c)
-        send(place(held), held, 2, across).wait_send()
-
-        @pl.when((zz >= z) & (z > 0))
-        def _():
-            send(place(held), held, 0, down).wait_send()
-
-        @pl.when((zz <= z) & (z < lines - 1))
-        def _():
-            send(place(held), held, 1, up).wait_send()
-
+        for h in range(2):
+            for yy in range(2):
+                send(index(zz, yy, 1 - c), h, 3).wait_recv()
+                send(index(zz, yy, c), h, 3).wait_send()
+            if h == 1:
+
+                @pl.when(buddy_z != zz)
+                def _():
+                    send(held, h, 2).wait_send()
+
+            else:
+                send(held, h, 2).wait_send()
+
+            @pl.when((zz >= z) & (z > 0))
+            def _():
+                send(held, h, 0).wait_send()
+
+            @pl.when((zz <= z) & (z < lines - 1))
+            def _():
+                send(held, h, 1).wait_send()
+
+    send(across, 1, 4).wait_send()
     own.wait()
 
 
@@ -362,8 +402,8 @@
         scratch_shapes=[
             pltpu.VMEM((8, feat), jnp.float32),
             pltpu.VMEM((tile_count, 8, feat), jnp.float32),
-            pltpu.SemaphoreType.DMA((4, tile_count)),
-            pltpu.SemaphoreType.DMA((tile_count,)),
+            pltpu.SemaphoreType.DMA((5, 2 * tile_count)),
+            pltpu.SemaphoreType.DMA((2 * tile_count,)),
             pltpu.SemaphoreType.DMA((tile_count,)),
             pltpu.SemaphoreType.DMA((tile_count,)),
             pltpu.SemaphoreType.DMA,
@@ -476,12 +516,10 @@
     own_index = lax.axis_index("tile")
     tile_local = grid_tokens.shape[0] // TILE_ROWS
     width = grid_tokens.shape[1]
-    my_counts = lax.dynamic_slice_in_dim(block_counts, own_index * tile_local, tile_local)
-    near = tile_count <= 16 and tile_count % 4 == 0
+    near = tile_count <= 16 and tile_count % 8 == 0
     if near:
         blocks, feat_mean, feat_rstd = gather_blocks(obs_features, tile_count)
-        my_lists = lax.dynamic_slice_in_dim(block_lists, own_index * tile_local, tile_local)
-        pick = jnp.take(block_position, my_lists.reshape(-1), axis=0)
+        lists, counts, position = block_lists, block_counts, block_position
     else:
         obs_wide = obs_features.astype(jnp.float32)
         first_sum, second_sum = lax.psum(
@@ -497,10 +535,15 @@
         blocks, pick = exchange(
             obs_features, block_lists, block_counts, block_position, tile_count, own_index
         )
+        lists = pick.reshape(tile_local, NSEL)
+        counts = lax.dynamic_slice_in_dim(block_counts, own_index * tile_local, tile_local)
+        position = jnp.arange(blocks.shape[0] // BLOCK, dtype=jnp.int32)
     encoded = attend(
         tile_count if near else 1,
-        pick,
-        my_counts,
+        near,
+        lists,
+        counts,
+        position,
         grid_tokens,
         blocks,
         feat_mean,

time: 117 us -> 114 us (0.974)
  local copies, waits for them, and re-layouts: 5.1 us -> 3.28 us
    pallas_call x1, Pallas kernels: 57.1 us -> 50.8 us  [gather_blocks(): pl.pallas_call(functools.partial(gather_kernel, tile_count // 4), out_sha...]
    pallas_call x1, Pallas kernels: 20 us -> 25.3 us  [scatter(): pl.pallas_call(functools.partial(scatter_kernel, count), out_shape=jax.Sh...]
    gather x1 -> x0, local copies, waits for them, and re-layouts: 1.64 us -> none  [local(): pick = jnp.take(block_position, my_lists.reshape(-1), axis=0)]
    dynamic_slice x3 -> x0, local copies, waits for them, and re-layouts: 1.41 us -> none  [the longest x1 1.26 us: local(): lax.dynamic_slice_in_dim(block_counts, own_index * tile_local, tile_local)]
    unnamed x3 -> x2, local copies, waits for them, and re-layouts: 1.87 us -> 3.28 us
where the time goes in v3:
time: 114 us; the launch traced here: 113 us
  Pallas kernels  110 us (96%)
  local copies, waits for them, and re-layouts  3.28 us (3%)
    pallas_call x1, Pallas kernels, gather_blocks(): pl.pallas_call(functools.partial(gather_kernel, tile_count // 4), out_sha...  50.8 us
    pallas_call x1, Pallas kernels, attend(): pl.pallas_call(functools.partial(attend_kernel, owned), grid_spec=pltpu.P...  33.8 us
    pallas_call x1, Pallas kernels, scatter(): pl.pallas_call(functools.partial(scatter_kernel, count), out_shape=jax.Sh...  25.3 us
    unnamed x2, local copies, waits for them, and re-layouts  3.28 us

profile of v3, /device:TPU:13, one launch (start us, length us, event | category | flops | bytes accessed | tf_op | source)
XLA Modules:
  0.0 113.2 jit_solution(1031905631575381177)
XLA Ops:
  0.0 1.4 %copy.13.list_ref = s32[64,32]{1,0:T(8,128)} copy(s32[64,32]{0,1:T(8,128)} %param.20) | data formatting | bytes 16384 | tf_op args[8]
  1.4 50.8 %shard_map.118 = (bf16[32768,128]{1,0:T(8,128)(2,1)}, f32[1,128]{1,0:T(1,128)}, f32[1,128]{1,0:T(1,128)}) custom-call(bf16[2048,128]{1,0:T(8,128)(2,1)} %obs_ref.1), custom_call_target="tpu_custom_call" | custom-call | tf_op jit(solution)/shard_map/pallas_call | solution.py:393
  52.2 33.8 %shard_map.119.encoded_ref = bf16[16,4,8,512]{3,2,1,0:T(8,128)(2,1)} custom-call(s32[64,32]{1,0:T(8,128)} %copy.13.list_ref, s32[64]{0:T(128)} %count_ref.1, s32[512]{0:T(512)} %position_ref.1, bf16[512,512]{1,0:T(8,128)(2,1)} %grid_ref.1, bf16[32768,128]{1,0:T(8,128)(2,1)} %get-tuple-element.8.blocks_ref, f32[1,128]{1,0:T(1,128)} %get-tuple-element.9.mean_ref, ...), custom_call_target="tpu_custom_call" | custom-call | flops 12000000000 | bytes 6000000 | tf_op jit(solution)/shard_map/pallas_call | solution.py:153
  86.0 25.3 %shard_map.120 = bf16[64,8,512]{2,1,0:T(8,128)(2,1)} custom-call(s32[64]{0:T(128)} %order_ref.1, bf16[16,4,8,512]{3,2,1,0:T(8,128)(2,1)} %shard_map.119.encoded_ref), custom_call_target="tpu_custom_call" | custom-call | tf_op jit(solution)/shard_map/pallas_call | solution.py:455
  111.3 1.9 %copy.15 = bf16[512,512]{1,0:T(8,128)(2,1)} copy(bf16[512,512]{1,0:T(8,128)(2,1)} %bitcast.2) | data formatting | bytes 1048576
